TPU v7x, 32 devices: a whole 2x2x4 slice. The times are simulated.
32 devices in a mesh: groups: 2 (over y), rows: 4 (over z), cams: 2 (over x), cols: 2 (over core).
Axes of the slice: x: 2, y: 2, z: 4, core: 2. Of those that a mesh axis runs over, the one named last changes fastest.
Arguments:
- left_feats: bfloat16 [4, 32, 1024, 128], P(('groups', 'cams'), 'rows', 'cols'), parts along dimension 0, may hold values from -6 to 6
- right_feats: bfloat16 [4, 32, 1024, 128], P(('groups', 'cams'), 'rows', 'cols'), parts along dimension 0, may hold values from -6 to 6
- prev_hidden: bfloat16 [4, 32, 1024, 128], P(('groups', 'cams'), 'rows', 'cols'), parts along dimension 0, may hold values from -1 to 1
- warp_list: int32 [4, 32, 8, 4], P(('groups', 'cams'), 'rows', 'cols'), parts along dimension 0, may hold values from -1 to 7, as said below
- enc_weight: bfloat16 [192, 128], replicated, may hold values from -0.4375 to 0.4375
- hgate_w: bfloat16 [5, 256, 256], replicated, may hold values from -0.15625 to 0.15625
- hcand_w: bfloat16 [5, 256, 128], replicated, may hold values from -0.15625 to 0.15625
- vgate_w: bfloat16 [5, 256, 256], replicated, may hold values from -0.15625 to 0.15625
- vcand_w: bfloat16 [5, 256, 128], replicated, may hold values from -0.15625 to 0.15625
Outputs:
- hidden_next: bfloat16 [4, 32, 1024, 128], P(('groups', 'cams'), 'rows', 'cols'), parts along dimension 0
There are 2 independent parts, one for each index of `groups`. A program takes and returns all parts, laid end to end along the dimension named above; an argument that names none is the same for every part. Nothing has to cross between parts.
Inputs may be any that keep to these rules, and one draw needn't show every extreme that they name: Entry 0 of warp_list is the band offset k, entry 1 the source row within a band of 8 rows, entry 2 the source block among the 4 blocks of the same column half, entry 3 the valid flag. Among the 32 blocks of one band and column half of one view, exactly half take offset 0 and a quarter each take -1 and 1, so at most 8 come from one neighbouring band, and the blocks that take one offset name distinct source blocks. The flag is 0 wherever the source band lies outside the image.
All inputs are finite; a program needn't handle non-finite values.
Results may differ from a plain program's by a relative error of at most 0.0062.
Values may be sent and summed in bfloat16 or wider, within the bound.
No kernel may reach another device: no remote copies, remote signals or barrier semaphores. Data moves between devices by JAX's collectives and lax.ppermute only.
A program may use at most 128 MiB of HBM per device.

v0:
```python
import functools

import jax
import jax.numpy as jnp
from jax import lax
from jax.experimental import pallas as pl
from jax.experimental.pallas import tpu as pltpu
from jax.sharding import PartitionSpec as P

bf16 = jnp.bfloat16
f32 = jnp.float32
SEAM = 16
VMEM_LIMIT = 56 << 20


def dotf(a, b):
    return jnp.dot(a, b, preferred_element_type=f32)


def sigmoid(v):
    return 0.5 * jnp.tanh(0.5 * v) + 0.5


def swap_near(value, axis):
    count = lax.axis_size(axis)
    pairs = [(i, i ^ 1) for i in range(count) if i ^ 1 < count]
    return lax.ppermute(value, axis, pairs)


def swap_far(value, axis):
    count = lax.axis_size(axis)
    pairs = []
    for i in range(1, count - 1, 2):
        pairs += [(i, i + 1), (i + 1, i)]
    return lax.ppermute(value, axis, pairs)


def whole(a):
    return pl.BlockSpec(a.shape, lambda *_: (0,) * a.ndim)


def motion_kernel(left_ref, right_ref, edge_ref, weight_ref, out_ref, window):
    disparities = weight_ref.shape[0]
    rows, width, feats = left_ref.shape
    tile = 128
    scale = feats**-0.5
    lane = lax.broadcasted_iota(jnp.int32, (tile, tile), 1)
    row = lax.broadcasted_iota(jnp.int32, (tile, tile), 0)
    keep = lane < row
    flip = (lane + row == tile - 1).astype(f32).astype(bf16)
    weight = weight_ref[...]
    for r in range(rows):
        window[r, pl.ds(0, disparities), :] = edge_ref[r]
        window[r, pl.ds(disparities, width), :] = right_ref[r]
    tiles = [(r, t * tile) for r in range(rows) for t in range(width // tile)]
    span = disparities + tile
    blocks = -(-span // tile)
    flipped = [dotf(flip, left_ref[r, pl.ds(x, tile), :]).astype(bf16) for r, x in tiles]
    scores = [
        lax.dot_general(
            part,
            window[r, pl.ds(x, blocks * tile), :],
            (((1,), (1,)), ((), ())),
            preferred_element_type=f32,
        )
        * scale
        for part, (r, x) in zip(flipped, tiles)
    ]
    skewed = []
    for score in scores:
        rolled = [
            pltpu.roll(score[:, tile * j : tile * (j + 1)], 0, 1, stride=1, stride_axis=0)
            for j in range(blocks)
        ]
        lanes = [
            jnp.where(keep, rolled[j], rolled[j + 1]).astype(bf16) for j in range(blocks - 1)
        ]
        skewed.append(jnp.concatenate(lanes, axis=1)[:, :disparities])
    motions = [dotf(part, weight).astype(bf16) for part in skewed]
    for part, (r, x) in zip(motions, tiles):
        out_ref[r, pl.ds(x, tile), :] = dotf(flip, part).astype(bf16)


def motion_of(left, right, edge, weight_flipped):
    rows, width, feats = left.shape
    disparities, hidden = weight_flipped.shape
    step = 4 if rows % 4 == 0 else 1
    block = lambda *shape: pl.BlockSpec((step,) + shape, lambda i: (i, 0, 0))
    return pl.pallas_call(
        motion_kernel,
        grid=(rows // step,),
        in_specs=[
            block(width, feats),
            block(width, feats),
            block(disparities, feats),
            whole(weight_flipped),
        ],
        out_specs=block(width, hidden),
        out_shape=jax.ShapeDtypeStruct((rows, width, hidden), bf16),
        scratch_shapes=[pltpu.VMEM((step, width + 256, feats), bf16)],
        compiler_params=pltpu.CompilerParams(vmem_limit_bytes=VMEM_LIMIT),
        name="motion",
    )(left, right, edge, weight_flipped)


def gather_kernel(sign_ref, near_ref, far_ref, prev_ref, out_near, out_far, sems):
    band_rows, band_blocks = near_ref.shape[1:3]
    slots = out_near.shape[0]
    width = out_near.shape[1]

    def copy(side, out, slot, row, block):
        return pltpu.make_async_copy(
            prev_ref.at[0, row, pl.ds(pl.multiple_of(block * width, width), width), :],
            out.at[slot],
            sems.at[side, slot],
        )

    sides = ((0, near_ref, out_near, sign_ref[0]), (1, far_ref, out_far, -sign_ref[0]))
    counts = []
    for side, list_ref, out, wanted in sides:

        def visit(i, count, side=side, list_ref=list_ref, out=out, wanted=wanted):
            row, block = i // band_blocks, i % band_blocks
            hit = (list_ref[0, row, block, 0] == wanted) & (count < slots)

            @pl.when(hit)
            def _():
                copy(side, out, count, list_ref[0, row, block, 1], list_ref[0, row, block, 2]).start()

            return count + hit.astype(jnp.int32)

        counts.append(lax.fori_loop(0, band_rows * band_blocks, visit, jnp.int32(0)))
    for side, list_ref, out, wanted in sides:

        @pl.loop(0, counts[side])
        def _(slot, side=side, out=out):
            copy(side, out, slot, 0, 0).wait()


def gather_blocks(sign, near_list, far_list, prev):
    band_rows, width, hidden = prev.shape[1:]
    band_blocks = near_list.shape[2]
    slots = band_rows * band_blocks // 4
    shape = jax.ShapeDtypeStruct((slots, width // band_blocks, hidden), bf16)
    smem = pl.BlockSpec(memory_space=pltpu.SMEM)
    anywhere = pl.BlockSpec(memory_space=pl.ANY)
    return pl.pallas_call(
        gather_kernel,
        in_specs=[smem, smem, smem, anywhere],
        out_specs=[anywhere, anywhere],
        out_shape=[shape, shape],
        scratch_shapes=[pltpu.SemaphoreType.DMA((2, slots))],
        name="gather",
    )(sign, near_list, far_list, prev)


def warp_kernel(sign_ref, list_ref, prev_ref, near_ref, far_ref, out_ref, zeros, sems):
    band_rows, band_blocks = list_ref.shape[1:3]
    slots, width = near_ref.shape[:2]
    zeros[...] = jnp.zeros_like(zeros)

    def visit(i, counts):
        row, block = i // band_blocks, i % band_blocks
        offset = list_ref[0, row, block, 0]
        valid = list_ref[0, row, block, 3] > 0
        target = out_ref.at[row, pl.ds(pl.multiple_of(block * width, width), width), :]
        is_near = offset == -sign_ref[0]
        is_far = offset == sign_ref[0]

        @pl.when(jnp.logical_not(valid))
        def _():
            pltpu.make_async_copy(zeros, target, sems.at[i]).start()

        @pl.when(valid & (offset == 0))
        def _():
            column = pl.multiple_of(list_ref[0, row, block, 2] * width, width)
            source = prev_ref.at[0, list_ref[0, row, block, 1], pl.ds(column, width), :]
            pltpu.make_async_copy(source, target, sems.at[i]).start()

        @pl.when(valid & is_near)
        def _():
            slot = jnp.minimum(counts[0], slots - 1)
            pltpu.make_async_copy(near_ref.at[slot], target, sems.at[i]).start()

        @pl.when(valid & is_far)
        def _():
            slot = jnp.minimum(counts[1], slots - 1)
            pltpu.make_async_copy(far_ref.at[slot], target, sems.at[i]).start()

        return counts[0] + is_near.astype(jnp.int32), counts[1] + is_far.astype(jnp.int32)

    lax.fori_loop(0, band_rows * band_blocks, visit, (jnp.int32(0), jnp.int32(0)))

    @pl.loop(0, band_rows * band_blocks)
    def _(i):
        row, block = i // band_blocks, i % band_blocks
        target = out_ref.at[row, pl.ds(pl.multiple_of(block * width, width), width), :]
        pltpu.make_async_copy(zeros, target, sems.at[i]).wait()


def warp_of(sign, warp_list, prev, near, far):
    band_rows, width, hidden = prev.shape[1:]
    band_blocks = warp_list.shape[2]
    smem = pl.BlockSpec(memory_space=pltpu.SMEM)
    anywhere = pl.BlockSpec(memory_space=pl.ANY)
    return pl.pallas_call(
        warp_kernel,
        in_specs=[smem, smem, anywhere, anywhere, anywhere],
        out_specs=anywhere,
        out_shape=jax.ShapeDtypeStruct((band_rows, width, hidden), bf16),
        scratch_shapes=[
            pltpu.VMEM((width // band_blocks, hidden), bf16),
            pltpu.SemaphoreType.DMA((band_rows * band_blocks,)),
        ],
        name="warp",
    )(sign, warp_list, prev, near, far)


def horizontal_kernel(
    place_ref, hidden_ref, motion_ref, seam_ref, gates_ref, cand_ref, out_ref, near_ref, far_ref,
    joined, reset, partial,
):
    rows, width, ch = hidden_ref.shape
    taps = gates_ref.shape[0]
    half = taps // 2
    right = place_ref[0]
    pad = SEAM
    own = pl.multiple_of(pad + pad * right, pad)
    seam = pl.multiple_of(pad + width * (1 - right), pad)
    span = width + SEAM
    gates = gates_ref[...].reshape(taps * 2 * ch, 2 * ch)
    for r in range(rows):
        for edge in (0, span + pad):
            joined[r, pl.ds(edge, pad), :] = jnp.zeros((pad, 2 * ch), bf16)
            reset[r, pl.ds(edge, pad), :] = jnp.zeros((pad, ch), bf16)
        joined[r, pl.ds(own, width), 0:ch] = hidden_ref[r]
        joined[r, pl.ds(own, width), ch : 2 * ch] = motion_ref[r]
        joined[r, pl.ds(seam, SEAM), :] = seam_ref[r]
    sums = [
        dotf(
            jnp.concatenate(
                [joined[r, pl.ds(pad - half + t, span), :] for t in range(taps)], axis=1
            ),
            gates,
        )
        for r in range(rows)
    ]
    update = []
    for r in range(rows):
        update.append(sigmoid(sums[r][:, :ch]))
        current = joined[r, pl.ds(pad, span), 0:ch].astype(f32)
        reset[r, pl.ds(pad, span), :] = (sigmoid(sums[r][:, ch:]) * current).astype(bf16)
    for r in range(rows):
        both = jnp.concatenate([reset[r], joined[r, :, ch : 2 * ch]], axis=1)
        for t in range(0, taps, 2):
            pair = jnp.concatenate([cand_ref[k] for k in range(t, min(t + 2, taps))], axis=1)
            partial[r, :, pl.ds(t * ch, pair.shape[1])] = dotf(both, pair)
    totals = []
    for r in range(rows):
        total = None
        for t in range(taps):
            part = partial[r, pl.ds(pad - half + t, span), pl.ds(t * ch, ch)]
            total = part if total is None else total + part
        totals.append(total)
    for r in range(rows):
        current = joined[r, pl.ds(pad, span), 0:ch].astype(f32)
        cand = jnp.tanh(totals[r])
        reset[r, pl.ds(pad, span), :] = ((1.0 - update[r]) * current + update[r] * cand).astype(bf16)
    for r in range(rows):
        out_ref[r] = reset[r, pl.ds(own, width), :]
    to_near = pl.program_id(0) == place_ref[1]

    @pl.when(to_near)
    def _():
        near_ref[...] = out_ref[...]

    @pl.when(jnp.logical_not(to_near))
    def _():
        far_ref[...] = out_ref[...]


def horizontal_pass(place, hidden, motion, seam, gates, cand):
    rows, width, ch = hidden.shape
    step = rows // 2
    taps = gates.shape[0]
    length = width + SEAM + 2 * SEAM
    block = lambda *shape: pl.BlockSpec((step,) + shape, lambda i, p: (i, 0, 0))
    kept = pl.BlockSpec((step, width, ch), lambda i, p: (0, 0, 0))
    half_band = jax.ShapeDtypeStruct((step, width, ch), bf16)
    return pl.pallas_call(
        horizontal_kernel,
        grid_spec=pltpu.PrefetchScalarGridSpec(
            num_scalar_prefetch=1,
            grid=(2,),
            in_specs=[
                block(width, ch),
                block(width, ch),
                block(SEAM, 2 * ch),
                whole(gates),
                whole(cand),
            ],
            out_specs=[block(width, ch), kept, kept],
            scratch_shapes=[
                pltpu.VMEM((step, length, 2 * ch), bf16),
                pltpu.VMEM((step, length, ch), bf16),
                pltpu.VMEM((step, length, taps * ch), f32),
            ],
        ),
        out_shape=[jax.ShapeDtypeStruct((rows, width, ch), bf16), half_band, half_band],
        compiler_params=pltpu.CompilerParams(vmem_limit_bytes=VMEM_LIMIT),
        name="horizontal",
    )(place, hidden, motion, seam, gates, cand)


def row_pair(taps):
    count = len(taps)
    none = jnp.zeros_like(taps[0])
    return jnp.concatenate(
        [
            jnp.concatenate(
                [taps[j] if j < count else none, taps[j - 1] if j > 0 else none], axis=1
            )
            for j in range(count + 1)
        ],
        axis=0,
    )


def vertical_kernel(
    place_ref, hidden_ref, motion_ref, hidden_near, hidden_far, motion_near, motion_far,
    gates_ref, cand_ref, out_ref, hidden_rim, motion_rim, reset_pair, cand_pair,
):
    rows, _, ch = hidden_ref.shape
    taps = gates_ref.shape[0]
    half = taps // 2
    rim = 2 * half
    near_below = place_ref[2]
    near, far = rim * near_below, rim - rim * near_below
    hidden_rim[pl.ds(near, rim)] = hidden_near[...]
    hidden_rim[pl.ds(far, rim)] = hidden_far[...]
    motion_rim[pl.ds(near, rim)] = motion_near[...]
    motion_rim[pl.ds(far, rim)] = motion_far[...]

    @pl.when(pl.program_id(0) == 0)
    def _():
        reset_pair[...] = row_pair([gates_ref[t][:, ch:] for t in range(taps)])
        cand_pair[...] = row_pair([cand_ref[t] for t in range(taps)])

    gates = gates_ref[...].reshape(taps * 2 * ch, 2 * ch)

    def row_of(own, rim_ref, y):
        if y < 0:
            return rim_ref[y + rim]
        return own[y] if y < rows else rim_ref[rim + y - rows]

    state = lambda y: row_of(hidden_ref, hidden_rim, y)
    flow = lambda y: row_of(motion_ref, motion_rim, y)

    def stack(first, last, source):
        return jnp.concatenate(
            [part for y in range(first, last + 1) for part in (source(y), flow(y))], axis=1
        )

    reset_sums, update = {}, []
    for y in (-half, rows):
        both = dotf(stack(y - half, y + half + 1, state), reset_pair[...])
        reset_sums[y], reset_sums[y + 1] = both[:, :ch], both[:, ch:]
    sums = [dotf(stack(y - half, y + half, state), gates) for y in range(rows)]
    for y in range(rows):
        update.append(sigmoid(sums[y][:, :ch]))
        reset_sums[y] = sums[y][:, ch:]
    reset = {
        y: (sigmoid(reset_sums[y]) * state(y).astype(f32)).astype(bf16)
        for y in range(-half, rows + half)
    }
    totals = []
    for y in range(0, rows, 2):
        both = dotf(stack(y - half, y + half + 1, lambda k: reset[k]), cand_pair[...])
        totals += [both[:, :ch], both[:, ch:]]
    for y in range(rows):
        cand = jnp.tanh(totals[y])
        blended = (1.0 - update[y]) * state(y).astype(f32) + update[y] * cand
        out_ref[0, y] = blended.astype(bf16)


def vertical_pass(place, hidden, motion, rims, gates, cand):
    rows, width, ch = hidden.shape
    taps = gates.shape[0]
    rim = rims[0].shape[0]
    tile = 256
    block = lambda count: pl.BlockSpec((count, tile, ch), lambda i, p: (0, i, 0))
    return pl.pallas_call(
        vertical_kernel,
        grid_spec=pltpu.PrefetchScalarGridSpec(
            num_scalar_prefetch=1,
            grid=(width // tile,),
            in_specs=[block(rows), block(rows)] + [block(rim)] * 4 + [whole(gates), whole(cand)],
            out_specs=pl.BlockSpec((1, rows, tile, ch), lambda i, p: (0, 0, i, 0)),
            scratch_shapes=[pltpu.VMEM((2 * rim, tile, ch), bf16)] * 2
            + [pltpu.VMEM(((taps + 1) * 2 * ch, 2 * ch), bf16)] * 2,
        ),
        out_shape=jax.ShapeDtypeStruct((1, rows, width, ch), bf16),
        compiler_params=pltpu.CompilerParams(vmem_limit_bytes=VMEM_LIMIT),
        name="vertical",
    )(place, hidden, motion, *rims, gates, cand)


def shards(
    left_feats, right_feats, prev_hidden, warp_list, enc_weight, hgate_w, hcand_w, vgate_w, vcand_w
):
    rows, width = prev_hidden.shape[1:3]
    disparities = enc_weight.shape[0]
    half = rows // 2
    odd = lax.axis_index("rows") % 2
    right = lax.axis_index("cols")
    place = jnp.stack([right, 1 - odd, 1 - odd]).astype(jnp.int32)
    sign = jnp.stack([1 - 2 * odd]).astype(jnp.int32)

    edge = lax.ppermute(right_feats[0, :, width - disparities :, :], "cols", [(0, 1)])
    near_list = swap_near(warp_list, "rows")
    far_list = swap_far(warp_list, "rows")
    motion = motion_of(left_feats[0], right_feats[0], edge, enc_weight[::-1])
    to_near, to_far = gather_blocks(sign, near_list, far_list, prev_hidden)
    near = swap_near(to_near, "rows")
    far = swap_far(to_far, "rows")
    low, high = motion[:half], motion[half:]
    motion_near = swap_near(jnp.where(odd == 0, high, low), "rows")
    motion_far = swap_far(jnp.where(odd == 0, low, high), "rows")
    warped = warp_of(sign, warp_list, prev_hidden, near, far)
    stacked = lambda at: jnp.concatenate(
        [warped[:, at : at + SEAM], motion[:, at : at + SEAM]], axis=2
    )
    seam = lax.ppermute(
        jnp.where(right == 0, stacked(width - SEAM), stacked(0)), "cols", [(0, 1), (1, 0)]
    )
    hidden, state_to_near, state_to_far = horizontal_pass(
        place, warped, motion, seam, hgate_w, hcand_w
    )
    state_near = swap_near(state_to_near, "rows")
    state_far = swap_far(state_to_far, "rows")
    return vertical_pass(
        place,
        hidden,
        motion,
        (state_near, state_far, motion_near, motion_far),
        vgate_w,
        vcand_w,
    )


def solution(mesh):
    spread = P(("groups", "cams"), "rows", "cols", None)
    return jax.shard_map(
        shards,
        mesh=mesh,
        in_specs=(spread,) * 4 + (P(),) * 5,
        out_specs=spread,
        check_vma=False,
    )
```

profile of v0, /device:TPU:8, one launch (start us, length us, event | category | flops | bytes accessed | tf_op | source)
XLA Modules:
  0.0 118.6 jit_solution(9195249552104178856)
XLA Ops:
  0.0 0.8 copy.12.list_ref
  0.8 3.5 %collective-permute-start.1 = (s32[1,8,4,4]{3,2,1,0:T(4,128)S(1)}, s32[1,8,4,4]{3,2,1,0:T(4,128)S(1)}, u32[]{:S(2)}, u32[]{:S(2)}) collective-permute-start(s32[1,8,4,4]{3,2,1,0:T(4,128)S(1)} %copy.12.list_ref), channel_id=1, source_target_pairs={{4,8},{8,4},{5,9},{9,5},{6,10},{10,6},{7,11},{11,7},{20,24},{24,20... | collective-permute-start | bytes 1544 | tf_op jit(solution)/shard_map/ppermute | solution.py:35
  4.3 0.1 collective-permute-start
  4.4 0.0 copy-done.7
  4.4 2.0 %collective-permute-done.1.far_ref = s32[1,8,4,4]{3,2,1,0:T(4,128)S(1)} collective-permute-done((s32[1,8,4,4]{3,2,1,0:T(4,128)S(1)}, s32[1,8,4,4]{3,2,1,0:T(4,128)S(1)}, u32[]{:S(2)}, u32[]{:S(2)}) %collective-permute-start.1) | collective-permute-done | bytes 544 | tf_op jit(solution)/shard_map/ppermute | solution.py:35
  6.4 1.7 %collective-permute-done.near_ref = s32[1,8,4,4]{3,2,1,0:T(4,128)S(1)} collective-permute-done((s32[1,8,4,4]{3,2,1,0:T(4,128)S(1)}, s32[1,8,4,4]{3,2,1,0:T(4,128)S(1)}, u32[]{:S(2)}, u32[]{:S(2)}) %collective-permute-start) | collective-permute-done | bytes 544 | tf_op jit(solution)/shard_map/ppermute | solution.py:27
  8.1 0.0 copy-done.10
  8.1 0.6 copy-done.11
  8.7 18.4 %gather.1 = (bf16[8,128,128]{2,1,0:T(8,128)(2,1)}, bf16[8,128,128]{2,1,0:T(8,128)(2,1)}) custom-call(s32[1]{0:T(128)} %bitcast.2.sign_ref, s32[1,8,4,4]{3,2,1,0:T(4,128)} %copy-done.11, s32[1,8,4,4]{3,2,1,0:T(4,128)} %copy-done.10, bf16[1,8,512,128]{3,2,1,0:T(8,128)(2,1)} %prev_ref.3), custom_call_target="tpu_custom_call" | custom-call | tf_op jit(solution)/shard_map/gather/pallas_call | solution.py:147
  27.1 0.1 collective-permute-start.2
  27.2 0.0 copy-start.9
  27.2 2.5 %collective-permute-start.3 = (bf16[8,128,128]{2,1,0:T(8,128)(2,1)}, bf16[8,128,128]{2,1,0:T(8,128)(2,1)S(1)}, u32[]{:S(2)}, u32[]{:S(2)}) collective-permute-start(bf16[8,128,128]{2,1,0:T(8,128)(2,1)} %get-tuple-element.11), channel_id=1, source_target_pairs={{4,8},{8,4},{5,9},{9,5},{6,10},{10,6},{7,11},{11,7},{20,24},{24,20... | collective-permute-start | bytes 786440 | tf_op jit(solution)/shard_map/ppermute | solution.py:35
  29.7 1.0 slice_bitcast_fusion
  30.7 1.3 %collective-permute-start.4 = (bf16[8,192,128]{2,1,0:T(8,128)(2,1)S(1)}, bf16[8,192,128]{2,1,0:T(8,128)(2,1)S(1)}, u32[]{:S(2)}, u32[]{:S(2)}) collective-permute-start(bf16[8,192,128]{2,1,0:T(8,128)(2,1)S(1)} %slice_bitcast_fusion), channel_id=1, source_target_pairs={{0,1},{2,3},{4,5},{6,7},{8,9},{10,11},{12,13},{14,15},{16,17},{18,... | collective-permute-start | bytes 1179656 | tf_op jit(solution)/shard_map/ppermute | solution.py:419
  32.1 0.0 copy-done.9
  32.1 0.7 rev.3.weight_ref
  32.8 0.6 pad_add_fusion.place_ref
  33.4 0.7 collective-permute-done.2.near_ref
  34.1 2.0 %collective-permute-done.3.far_ref = bf16[8,128,128]{2,1,0:T(8,128)(2,1)S(1)} collective-permute-done((bf16[8,128,128]{2,1,0:T(8,128)(2,1)}, bf16[8,128,128]{2,1,0:T(8,128)(2,1)S(1)}, u32[]{:S(2)}, u32[]{:S(2)}) %collective-permute-start.3) | collective-permute-done | bytes 262176 | tf_op jit(solution)/shard_map/ppermute | solution.py:35
  36.2 0.0 copy-done.5
  36.2 0.7 copy-done.6
  36.9 33.1 %warp.1.hidden_ref = bf16[8,512,128]{2,1,0:T(8,128)(2,1)} custom-call(s32[1]{0:T(128)} %bitcast.2.sign_ref, s32[1,8,4,4]{3,2,1,0:T(4,128)} %copy-done.7, bf16[1,8,512,128]{3,2,1,0:T(8,128)(2,1)} %prev_ref.3, bf16[8,128,128]{2,1,0:T(8,128)(2,1)} %copy-done.5, bf16[8,128,128]{2,1,0:T(8,128)(2,1)} %copy-done.6), custom_call_target="tpu_custom_call" | custom-call | tf_op jit(solution)/shard_map/warp/pallas_call | solution.py:206
  70.0 0.8 fusion
  70.8 0.0 collective-permute-done.4.edge_ref
  70.8 0.0 copy-start.4
  70.8 0.7 copy-done.4
  71.5 5.1 %motion.1.motion_ref = bf16[8,512,128]{2,1,0:T(8,128)(2,1)} custom-call(bf16[8,512,128]{2,1,0:T(8,128)(2,1)} %bitcast.8, bf16[8,512,128]{2,1,0:T(8,128)(2,1)} %bitcast.7, bf16[8,192,128]{2,1,0:T(8,128)(2,1)} %copy-done.4, bf16[192,128]{1,0:T(8,128)(2,1)} %rev.3.weight_ref), custom_call_target="tpu_custom_call" | custom-call | tf_op jit(solution)/shard_map/motion/pallas_call | solution.py:89
  76.7 0.8 fusion.1
  77.5 0.1 collective-permute-start.5
  77.5 1.3 %broadcast_select_fusion = (bf16[4,512,128]{2,1,0:T(8,128)(2,1)S(1)}, bf16[4,512,128]{2,1,0:T(8,128)(2,1)S(1)}) fusion(pred[]{:T(512)S(6)} %eq.10, bf16[8,512,128]{2,1,0:T(8,128)(2,1)} %motion.1.motion_ref), kind=kLoop, calls=%fused_computation | loop fusion | flops 524288 | bytes 2097153 | tf_op jit(solution)/shard_map/jit(_where)/select_n | solution.py:428
  78.8 1.9 %collective-permute-start.9 = (bf16[4,512,128]{2,1,0:T(8,128)(2,1)S(1)}, bf16[4,512,128]{2,1,0:T(8,128)(2,1)S(1)}, u32[]{:S(2)}, u32[]{:S(2)}) collective-permute-start(bf16[4,512,128]{2,1,0:T(8,128)(2,1)S(1)} %get-tuple-element.15), channel_id=1, source_target_pairs={{4,8},{8,4},{5,9},{9,5},{6,10},{10,6},{7,11},{11,7},{20,24},{24,20... | collective-permute-start | bytes 1572872 | tf_op jit(solution)/shard_map/ppermute | solution.py:35
  80.7 0.1 collective-permute-start.8
  80.8 0.0 collective-permute-done.5.seam_ref
  80.8 0.0 copy-start.8
  80.8 0.6 copy-done.8
  81.5 9.4 %horizontal.1 = (bf16[8,512,128]{2,1,0:T(8,128)(2,1)}, bf16[4,512,128]{2,1,0:T(8,128)(2,1)}, bf16[4,512,128]{2,1,0:T(8,128)(2,1)}) custom-call(s32[3]{0:T(128)} %pad_add_fusion.place_ref, bf16[8,512,128]{2,1,0:T(8,128)(2,1)} %warp.1.hidden_ref, bf16[8,512,128]{2,1,0:T(8,128)(2,1)} %motion.1.motion_ref, bf16[8,16,256]{2,1,0:T(8,128)(2,1)} %copy-done.8, ...), custom_call_target="tpu_custom_call" | custom-call | tf_op jit(solution)/shard_map/horizontal/pallas_call | solution.py:290
  90.9 2.0 %collective-permute-start.6 = (bf16[4,512,128]{2,1,0:T(8,128)(2,1)}, bf16[4,512,128]{2,1,0:T(8,128)(2,1)S(1)}, u32[]{:S(2)}, u32[]{:S(2)}) collective-permute-start(bf16[4,512,128]{2,1,0:T(8,128)(2,1)} %get-tuple-element.13), channel_id=1, source_target_pairs={{0,4},{4,0},{8,12},{12,8},{1,5},{5,1},{9,13},{13,9},{2,6},{6,2},{1... | collective-permute-start | bytes 1572872 | tf_op jit(solution)/shard_map/ppermute | solution.py:27
  92.9 3.9 %collective-permute-start.7 = (bf16[4,512,128]{2,1,0:T(8,128)(2,1)}, bf16[4,512,128]{2,1,0:T(8,128)(2,1)S(1)}, u32[]{:S(2)}, u32[]{:S(2)}) collective-permute-start(bf16[4,512,128]{2,1,0:T(8,128)(2,1)} %get-tuple-element.14), channel_id=1, source_target_pairs={{4,8},{8,4},{5,9},{9,5},{6,10},{10,6},{7,11},{11,7},{20,24},{24,20... | collective-permute-start | bytes 1572872 | tf_op jit(solution)/shard_map/ppermute | solution.py:35
  96.8 0.0 collective-permute-done.9.motion_far
  96.8 0.0 copy-start
  96.8 0.0 collective-permute-done.8.motion_near
  96.8 0.0 copy-start.1
  96.8 9.5 %collective-permute-done.6.hidden_near = bf16[4,512,128]{2,1,0:T(8,128)(2,1)S(1)} collective-permute-done((bf16[4,512,128]{2,1,0:T(8,128)(2,1)}, bf16[4,512,128]{2,1,0:T(8,128)(2,1)S(1)}, u32[]{:S(2)}, u32[]{:S(2)}) %collective-permute-start.6) | collective-permute-done | bytes 524320 | tf_op jit(solution)/shard_map/ppermute | solution.py:27
  106.4 2.4 %collective-permute-done.7.hidden_far = bf16[4,512,128]{2,1,0:T(8,128)(2,1)S(1)} collective-permute-done((bf16[4,512,128]{2,1,0:T(8,128)(2,1)}, bf16[4,512,128]{2,1,0:T(8,128)(2,1)S(1)}, u32[]{:S(2)}, u32[]{:S(2)}) %collective-permute-start.7) | collective-permute-done | bytes 524320 | tf_op jit(solution)/shard_map/ppermute | solution.py:35
  108.7 0.0 copy-done
  108.8 0.0 copy-done.1
  108.8 0.8 copy-done.3
  109.5 9.1 %vertical.1 = bf16[1,8,512,128]{3,2,1,0:T(8,128)(2,1)} custom-call(s32[3]{0:T(128)} %pad_add_fusion.place_ref, bf16[8,512,128]{2,1,0:T(8,128)(2,1)} %get-tuple-element.12.hidden_ref, bf16[8,512,128]{2,1,0:T(8,128)(2,1)} %motion.1.motion_ref, bf16[4,512,128]{2,1,0:T(8,128)(2,1)} %copy-done.2, bf16[4,512,128]{2,1,0:T(8,128)(2,1)} %copy-done.3, ...), custom_call_target="tpu_custom_call" | custom-call | tf_op jit(solution)/shard_map/vertical/pallas_call | solution.py:392
  (9 shorter events, 0.0 us)
Async XLA Ops:
  0.8 3.6 %copy-start.7 = (s32[1,8,4,4]{3,2,1,0:T(4,128)}, s32[1,8,4,4]{3,2,1,0:T(4,128)S(1)}, u32[]{:S(2)}) copy-start(s32[1,8,4,4]{3,2,1,0:T(4,128)S(1)} %copy.12.list_ref) | copy-start | bytes 1540
  0.8 5.6 %collective-permute-start.1 = (s32[1,8,4,4]{3,2,1,0:T(4,128)S(1)}, s32[1,8,4,4]{3,2,1,0:T(4,128)S(1)}, u32[]{:S(2)}, u32[]{:S(2)}) collective-permute-start(s32[1,8,4,4]{3,2,1,0:T(4,128)S(1)} %copy.12.list_ref), channel_id=1, source_target_pairs={{4,8},{8,4},{5,9},{9,5},{6,10},{10,6},{7,11},{11,7},{20,24},{24,20... | collective-permute-start | bytes 1544 | tf_op jit(solution)/shard_map/ppermute | solution.py:35
  4.3 3.8 %collective-permute-start = (s32[1,8,4,4]{3,2,1,0:T(4,128)S(1)}, s32[1,8,4,4]{3,2,1,0:T(4,128)S(1)}, u32[]{:S(2)}, u32[]{:S(2)}) collective-permute-start(s32[1,8,4,4]{3,2,1,0:T(4,128)S(1)} %copy.12.list_ref), channel_id=1, source_target_pairs={{0,4},{4,0},{8,12},{12,8},{1,5},{5,1},{9,13},{13,9},{2,6},{6,2},{1... | collective-permute-start | bytes 1544 | tf_op jit(solution)/shard_map/ppermute | solution.py:27
  6.4 1.7 %copy-start.10 = (s32[1,8,4,4]{3,2,1,0:T(4,128)}, s32[1,8,4,4]{3,2,1,0:T(4,128)S(1)}, u32[]{:S(2)}) copy-start(s32[1,8,4,4]{3,2,1,0:T(4,128)S(1)} %collective-permute-done.1.far_ref) | copy-start | bytes 1540
  8.1 0.6 copy-start.11
  27.1 7.0 %collective-permute-start.2 = (bf16[8,128,128]{2,1,0:T(8,128)(2,1)}, bf16[8,128,128]{2,1,0:T(8,128)(2,1)S(1)}, u32[]{:S(2)}, u32[]{:S(2)}) collective-permute-start(bf16[8,128,128]{2,1,0:T(8,128)(2,1)} %get-tuple-element.10), channel_id=1, source_target_pairs={{0,4},{4,0},{8,12},{12,8},{1,5},{5,1},{9,13},{13,9},{2,6},{6,2},{1... | collective-permute-start | bytes 786440 | tf_op jit(solution)/shard_map/ppermute | solution.py:27
  27.2 4.9 %copy-start.9 = (bf16[192,128]{1,0:T(8,128)(2,1)S(1)}, bf16[192,128]{1,0:T(8,128)(2,1)}, u32[]{:S(2)}) copy-start(bf16[192,128]{1,0:T(8,128)(2,1)} %param.13) | copy-start | bytes 147460
  27.2 9.0 %collective-permute-start.3 = (bf16[8,128,128]{2,1,0:T(8,128)(2,1)}, bf16[8,128,128]{2,1,0:T(8,128)(2,1)S(1)}, u32[]{:S(2)}, u32[]{:S(2)}) collective-permute-start(bf16[8,128,128]{2,1,0:T(8,128)(2,1)} %get-tuple-element.11), channel_id=1, source_target_pairs={{4,8},{8,4},{5,9},{9,5},{6,10},{10,6},{7,11},{11,7},{20,24},{24,20... | collective-permute-start | bytes 786440 | tf_op jit(solution)/shard_map/ppermute | solution.py:35
  30.7 40.1 %collective-permute-start.4 = (bf16[8,192,128]{2,1,0:T(8,128)(2,1)S(1)}, bf16[8,192,128]{2,1,0:T(8,128)(2,1)S(1)}, u32[]{:S(2)}, u32[]{:S(2)}) collective-permute-start(bf16[8,192,128]{2,1,0:T(8,128)(2,1)S(1)} %slice_bitcast_fusion), channel_id=1, source_target_pairs={{0,1},{2,3},{4,5},{6,7},{8,9},{10,11},{12,13},{14,15},{16,17},{18,... | collective-permute-start | bytes 1179656 | tf_op jit(solution)/shard_map/ppermute | solution.py:419
  34.1 2.1 %copy-start.5 = (bf16[8,128,128]{2,1,0:T(8,128)(2,1)}, bf16[8,128,128]{2,1,0:T(8,128)(2,1)S(1)}, u32[]{:S(2)}) copy-start(bf16[8,128,128]{2,1,0:T(8,128)(2,1)S(1)} %collective-permute-done.2.near_ref) | copy-start | bytes 786436
  36.2 0.7 copy-start.6
  70.8 0.7 copy-start.4
  77.5 3.4 %collective-permute-start.5 = (bf16[8,16,256]{2,1,0:T(8,128)(2,1)S(1)}, bf16[8,16,256]{2,1,0:T(8,128)(2,1)S(1)}, u32[]{:S(2)}, u32[]{:S(2)}) collective-permute-start(bf16[8,16,256]{2,1,0:T(8,128)(2,1)S(1)} %maximum_select_fusion), channel_id=1, source_target_pairs={{0,1},{1,0},{2,3},{3,2},{4,5},{5,4},{6,7},{7,6},{8,9},{9,8},{10,11... | collective-permute-start | bytes 196616 | tf_op jit(solution)/shard_map/ppermute | solution.py:433
  78.8 18.0 %collective-permute-start.9 = (bf16[4,512,128]{2,1,0:T(8,128)(2,1)S(1)}, bf16[4,512,128]{2,1,0:T(8,128)(2,1)S(1)}, u32[]{:S(2)}, u32[]{:S(2)}) collective-permute-start(bf16[4,512,128]{2,1,0:T(8,128)(2,1)S(1)} %get-tuple-element.15), channel_id=1, source_target_pairs={{4,8},{8,4},{5,9},{9,5},{6,10},{10,6},{7,11},{11,7},{20,24},{24,20... | collective-permute-start | bytes 1572872 | tf_op jit(solution)/shard_map/ppermute | solution.py:35
  80.7 16.1 %collective-permute-start.8 = (bf16[4,512,128]{2,1,0:T(8,128)(2,1)S(1)}, bf16[4,512,128]{2,1,0:T(8,128)(2,1)S(1)}, u32[]{:S(2)}, u32[]{:S(2)}) collective-permute-start(bf16[4,512,128]{2,1,0:T(8,128)(2,1)S(1)} %get-tuple-element.16), channel_id=1, source_target_pairs={{0,4},{4,0},{8,12},{12,8},{1,5},{5,1},{9,13},{13,9},{2,6},{6,2},{1... | collective-permute-start | bytes 1572872 | tf_op jit(solution)/shard_map/ppermute | solution.py:27
  80.8 0.6 copy-start.8
  90.9 15.5 %collective-permute-start.6 = (bf16[4,512,128]{2,1,0:T(8,128)(2,1)}, bf16[4,512,128]{2,1,0:T(8,128)(2,1)S(1)}, u32[]{:S(2)}, u32[]{:S(2)}) collective-permute-start(bf16[4,512,128]{2,1,0:T(8,128)(2,1)} %get-tuple-element.13), channel_id=1, source_target_pairs={{0,4},{4,0},{8,12},{12,8},{1,5},{5,1},{9,13},{13,9},{2,6},{6,2},{1... | collective-permute-start | bytes 1572872 | tf_op jit(solution)/shard_map/ppermute | solution.py:27
  92.9 15.9 %collective-permute-start.7 = (bf16[4,512,128]{2,1,0:T(8,128)(2,1)}, bf16[4,512,128]{2,1,0:T(8,128)(2,1)S(1)}, u32[]{:S(2)}, u32[]{:S(2)}) collective-permute-start(bf16[4,512,128]{2,1,0:T(8,128)(2,1)} %get-tuple-element.14), channel_id=1, source_target_pairs={{4,8},{8,4},{5,9},{9,5},{6,10},{10,6},{7,11},{11,7},{20,24},{24,20... | collective-permute-start | bytes 1572872 | tf_op jit(solution)/shard_map/ppermute | solution.py:35
  96.8 11.9 %copy-start = (bf16[4,512,128]{2,1,0:T(8,128)(2,1)}, bf16[4,512,128]{2,1,0:T(8,128)(2,1)S(1)}, u32[]{:S(2)}) copy-start(bf16[4,512,128]{2,1,0:T(8,128)(2,1)S(1)} %collective-permute-done.9.motion_far) | copy-start | bytes 1572868
  96.8 11.9 %copy-start.1 = (bf16[4,512,128]{2,1,0:T(8,128)(2,1)}, bf16[4,512,128]{2,1,0:T(8,128)(2,1)S(1)}, u32[]{:S(2)}) copy-start(bf16[4,512,128]{2,1,0:T(8,128)(2,1)S(1)} %collective-permute-done.8.motion_near) | copy-start | bytes 1572868
  106.4 2.4 %copy-start.2 = (bf16[4,512,128]{2,1,0:T(8,128)(2,1)}, bf16[4,512,128]{2,1,0:T(8,128)(2,1)S(1)}, u32[]{:S(2)}) copy-start(bf16[4,512,128]{2,1,0:T(8,128)(2,1)S(1)} %collective-permute-done.6.hidden_near) | copy-start | bytes 1572868
  108.7 0.8 copy-start.3
where the time goes:
time: 119 us
  Pallas kernels  75.1 us (63%)
  waiting for transfers between devices  18.3 us (15%)
  starting transfers between devices  15.4 us (13%)
  local copies, waits for them, and re-layouts  7.6 us (6%)
  other arithmetic  1.93 us (2%)
    pallas_call x1, Pallas kernels, warp_of(): pl.pallas_call(warp_kernel, in_specs=[smem, smem, anywhere, anywhere, any...  33.1 us
    pallas_call x1, Pallas kernels, gather_blocks(): pl.pallas_call(gather_kernel, in_specs=[smem, smem, smem, anywhere], out_...  18.4 us
    ppermute x4, waiting for transfers between devices, swap_near(): return lax.ppermute(value, axis, pairs)  11.9 us
    ppermute x4, starting transfers between devices, swap_far(): return lax.ppermute(value, axis, pairs)  11.8 us
    pallas_call x1, Pallas kernels, horizontal_pass(): pl.pallas_call(horizontal_kernel, grid_spec=pltpu.PrefetchScalarGridSpec(...  9.42 us
    pallas_call x1, Pallas kernels, vertical_pass(): pl.pallas_call(vertical_kernel, grid_spec=pltpu.PrefetchScalarGridSpec(nu...  9.12 us
    ppermute x4, waiting for transfers between devices, swap_far(): return lax.ppermute(value, axis, pairs)  6.46 us
    pallas_call x1, Pallas kernels, motion_of(): pl.pallas_call(motion_kernel, grid=(rows // step,), in_specs=[block(width...  5.13 us
  transfers between devices with their start and end apart: 10, of which 6 were waited for; matrix products, arithmetic and copies ran while one was open for 4% of the time, Pallas kernels for 36%

commit v1 on v0

v1 whole, which is shorter than its diff:
```python
import functools

import jax
import jax.numpy as jnp
from jax import lax
from jax.experimental import pallas as pl
from jax.experimental.pallas import tpu as pltpu
from jax.sharding import PartitionSpec as P

bf16 = jnp.bfloat16
f32 = jnp.float32
SEAM = 16


def dotf(a, b):
    return jnp.dot(a, b, preferred_element_type=f32)


def sigmoid(v):
    return 0.5 * jnp.tanh(0.5 * v) + 0.5


def swap_near(value, axis):
    count = lax.axis_size(axis)
    pairs = [(i, i ^ 1) for i in range(count) if i ^ 1 < count]
    return lax.ppermute(value, axis, pairs)


def swap_far(value, axis):
    count = lax.axis_size(axis)
    pairs = []
    for i in range(1, count - 1, 2):
        pairs += [(i, i + 1), (i + 1, i)]
    return lax.ppermute(value, axis, pairs)


IN_VMEM = pl.BlockSpec(memory_space=pltpu.VMEM)
IN_SMEM = pl.BlockSpec(memory_space=pltpu.SMEM)


def params(megabytes):
    return pltpu.CompilerParams(vmem_limit_bytes=megabytes << 20)


def motion_kernel(
    place_ref, left_ref, right_ref, edge_ref, weight_ref, out_ref, near_ref, far_ref, window
):
    disparities = weight_ref.shape[0]
    _, rows, width, feats = left_ref.shape
    tile = 128
    scale = feats**-0.5
    lane = lax.broadcasted_iota(jnp.int32, (tile, tile), 1)
    row = lax.broadcasted_iota(jnp.int32, (tile, tile), 0)
    keep = lane < row
    flip = (lane + row == tile - 1).astype(f32).astype(bf16)
    turned = jnp.concatenate(
        [dotf(flip, weight_ref[pl.ds(disparities - tile, tile), :]).astype(bf16),
         dotf(flip, weight_ref[pl.ds(0, tile), :]).astype(bf16)[2 * tile - disparities :, :]],
        axis=0,
    )
    span = disparities + tile
    blocks = -(-span // tile)
    far_edge = edge_ref.shape[2] - disparities
    group = rows // 2
    for first in range(0, rows, group):
        own = range(first, first + group)
        for r in own:
            window[r, pl.ds(0, disparities), :] = edge_ref[0, r, pl.ds(far_edge, disparities), :]
            window[r, pl.ds(disparities, width), :] = right_ref[0, r]
        tiles = [(r, t * tile) for r in own for t in range(width // tile)]
        flipped = [dotf(flip, left_ref[0, r, pl.ds(x, tile), :]).astype(bf16) for r, x in tiles]
        scores = [
            lax.dot_general(
                part,
                window[r, pl.ds(x, blocks * tile), :],
                (((1,), (1,)), ((), ())),
                preferred_element_type=f32,
            )
            * scale
            for part, (r, x) in zip(flipped, tiles)
        ]
        skewed = []
        for score in scores:
            rolled = [
                pltpu.roll(score[:, tile * j : tile * (j + 1)], 0, 1, stride=1, stride_axis=0)
                for j in range(blocks)
            ]
            lanes = [
                jnp.where(keep, rolled[j], rolled[j + 1]).astype(bf16) for j in range(blocks - 1)
            ]
            skewed.append(jnp.concatenate(lanes, axis=1)[:, :disparities])
        motions = [dotf(part, turned).astype(bf16) for part in skewed]
        for part, (r, x) in zip(motions, tiles):
            out_ref[r, pl.ds(x, tile), :] = dotf(flip, part).astype(bf16)
    half = rows // 2
    near_ref[...] = out_ref[pl.ds(half * place_ref[1], half)]
    far_ref[...] = out_ref[pl.ds(half - half * place_ref[1], half)]


def motion_of(place, left, right, edge, weight):
    _, rows, width, feats = left.shape
    hidden = weight.shape[1]
    half_band = jax.ShapeDtypeStruct((rows // 2, width, hidden), bf16)
    return pl.pallas_call(
        motion_kernel,
        in_specs=[IN_SMEM] + [IN_VMEM] * 4,
        out_specs=[IN_VMEM] * 3,
        out_shape=[jax.ShapeDtypeStruct((rows, width, hidden), bf16), half_band, half_band],
        scratch_shapes=[pltpu.VMEM((rows, width + 256, feats), bf16)],
        compiler_params=params(24),
        name="motion",
    )(place, left, right, edge, weight)


def gather_kernel(place_ref, near_list, far_list, prev_ref, near_out, far_out, near_ref, far_ref, sems):
    copies = [
        pltpu.make_async_copy(near_list, near_ref, sems.at[0]),
        pltpu.make_async_copy(far_list, far_ref, sems.at[1]),
    ]
    for copy in copies:
        copy.start()
    for copy in copies:
        copy.wait()
    _, band_blocks, _, band_rows = near_ref.shape
    slots, width, _ = near_out.shape
    sign = 2 * place_ref[1] - 1
    for list_ref, out, wanted in ((near_ref, near_out, sign), (far_ref, far_out, -sign)):

        def visit(i, count, list_ref=list_ref, out=out, wanted=wanted):
            row, block = i // band_blocks, i % band_blocks
            hit = (list_ref[0, block, 0, row] == wanted) & (count < slots)

            @pl.when(hit)
            def _():
                column = pl.multiple_of(list_ref[0, block, 2, row] * width, width)
                out[count] = prev_ref[0, list_ref[0, block, 1, row], pl.ds(column, width), :]

            return count + hit.astype(jnp.int32)

        lax.fori_loop(0, band_rows * band_blocks, visit, jnp.int32(0))


def gather_blocks(place, near_list, far_list, prev):
    _, band_blocks, _, band_rows = near_list.shape
    _, _, width, hidden = prev.shape
    slots = band_rows * band_blocks // 4
    shape = jax.ShapeDtypeStruct((slots, width // band_blocks, hidden), bf16)
    return pl.pallas_call(
        gather_kernel,
        in_specs=[IN_SMEM, IN_VMEM, IN_VMEM, IN_VMEM],
        out_specs=[IN_VMEM, IN_VMEM],
        out_shape=[shape, shape],
        scratch_shapes=[pltpu.SMEM(near_list.shape, jnp.int32)] * 2
        + [pltpu.SemaphoreType.DMA((2,))],
        compiler_params=params(4),
        name="gather",
    )(place, near_list, far_list, prev)


def warp_kernel(place_ref, list_ref, prev_ref, near_ref, far_ref, motion_ref, out_ref, seam_ref):
    _, band_blocks, _, band_rows = list_ref.shape
    slots, width, ch = near_ref.shape
    sign = 2 * place_ref[1] - 1
    nears, fars = jnp.int32(0), jnp.int32(0)
    for row in range(band_rows):
        for block in range(band_blocks):
            offset = list_ref[0, block, 0, row]
            is_near, is_far = offset == -sign, offset == sign
            column = pl.multiple_of(list_ref[0, block, 2, row] * width, width)
            local = prev_ref[0, list_ref[0, block, 1, row], pl.ds(column, width), :]
            near = near_ref[jnp.minimum(nears, slots - 1)]
            far = far_ref[jnp.minimum(fars, slots - 1)]
            picked = jnp.where(is_near, near, jnp.where(is_far, far, local))
            picked = jnp.where(list_ref[0, block, 3, row] > 0, picked, jnp.zeros_like(picked))
            out_ref[row, pl.ds(block * width, width), :] = picked
            nears += is_near.astype(jnp.int32)
            fars += is_far.astype(jnp.int32)
    total = out_ref.shape[1]
    edge = pl.multiple_of((total - SEAM) * (1 - place_ref[0]), SEAM)
    for row in range(band_rows):
        seam_ref[row, :, 0:ch] = out_ref[row, pl.ds(edge, SEAM), :]
        seam_ref[row, :, ch : 2 * ch] = motion_ref[row, pl.ds(edge, SEAM), :]


def warp_of(place, warp_list, prev, near, far, motion):
    _, rows, width, ch = prev.shape
    return pl.pallas_call(
        warp_kernel,
        in_specs=[IN_SMEM, IN_SMEM] + [IN_VMEM] * 4,
        out_specs=[IN_VMEM, IN_VMEM],
        out_shape=[
            jax.ShapeDtypeStruct((rows, width, ch), bf16),
            jax.ShapeDtypeStruct((rows, SEAM, 2 * ch), bf16),
        ],
        compiler_params=params(4),
        name="warp",
    )(place, warp_list, prev, near, far, motion)


def horizontal_kernel(
    place_ref, hidden_ref, motion_ref, seam_ref, gates_ref, cand_ref, out_ref, near_ref, far_ref,
    joined, reset, partial,
):
    band_rows, width, ch = hidden_ref.shape
    taps = gates_ref.shape[0]
    half = taps // 2
    right = place_ref[0]
    pad = SEAM
    own = pl.multiple_of(pad + pad * right, pad)
    seam = pl.multiple_of(pad + width * (1 - right), pad)
    span = width + SEAM
    gates = gates_ref[...].reshape(taps * 2 * ch, 2 * ch)
    group = joined.shape[0]
    rows = range(group)
    for first in range(0, band_rows, group):
        for r in rows:
            for edge in (0, span + pad):
                joined[r, pl.ds(edge, pad), :] = jnp.zeros((pad, 2 * ch), bf16)
                reset[r, pl.ds(edge, pad), :] = jnp.zeros((pad, ch), bf16)
            joined[r, pl.ds(own, width), 0:ch] = hidden_ref[first + r]
            joined[r, pl.ds(own, width), ch : 2 * ch] = motion_ref[first + r]
            joined[r, pl.ds(seam, SEAM), :] = seam_ref[first + r]
        sums = [
            dotf(
                jnp.concatenate(
                    [joined[r, pl.ds(pad - half + t, span), :] for t in range(taps)], axis=1
                ),
                gates,
            )
            for r in rows
        ]
        update = []
        for r in rows:
            update.append(sigmoid(sums[r][:, :ch]))
            current = joined[r, pl.ds(pad, span), 0:ch].astype(f32)
            reset[r, pl.ds(pad, span), :] = (sigmoid(sums[r][:, ch:]) * current).astype(bf16)
        for r in rows:
            both = jnp.concatenate([reset[r], joined[r, :, ch : 2 * ch]], axis=1)
            for t in range(0, taps, 2):
                pair = jnp.concatenate([cand_ref[k] for k in range(t, min(t + 2, taps))], axis=1)
                partial[r, :, pl.ds(t * ch, pair.shape[1])] = dotf(both, pair)
        totals = []
        for r in rows:
            total = None
            for t in range(taps):
                part = partial[r, pl.ds(pad - half + t, span), pl.ds(t * ch, ch)]
                total = part if total is None else total + part
            totals.append(total)
        for r in rows:
            current = joined[r, pl.ds(pad, span), 0:ch].astype(f32)
            cand = jnp.tanh(totals[r])
            blended = (1.0 - update[r]) * current + update[r] * cand
            reset[r, pl.ds(pad, span), :] = blended.astype(bf16)
        for r in rows:
            out_ref[first + r] = reset[r, pl.ds(own, width), :]
    count = band_rows // 2
    near_ref[...] = out_ref[pl.ds(count * place_ref[1], count)]
    far_ref[...] = out_ref[pl.ds(count - count * place_ref[1], count)]


def horizontal_pass(place, hidden, motion, seam, gates, cand):
    rows, width, ch = hidden.shape
    group = rows // 2
    taps = gates.shape[0]
    length = width + SEAM + 2 * SEAM
    half_band = jax.ShapeDtypeStruct((rows // 2, width, ch), bf16)
    return pl.pallas_call(
        horizontal_kernel,
        in_specs=[IN_SMEM] + [IN_VMEM] * 5,
        out_specs=[IN_VMEM] * 3,
        out_shape=[jax.ShapeDtypeStruct((rows, width, ch), bf16), half_band, half_band],
        scratch_shapes=[
            pltpu.VMEM((group, length, 2 * ch), bf16),
            pltpu.VMEM((group, length, ch), bf16),
            pltpu.VMEM((group, length, taps * ch), f32),
        ],
        compiler_params=params(24),
        name="horizontal",
    )(place, hidden, motion, seam, gates, cand)


def row_pair(taps):
    count = len(taps)
    none = jnp.zeros_like(taps[0])
    return jnp.concatenate(
        [
            jnp.concatenate(
                [taps[j] if j < count else none, taps[j - 1] if j > 0 else none], axis=1
            )
            for j in range(count + 1)
        ],
        axis=0,
    )


def vertical_kernel(
    place_ref, hidden_ref, motion_ref, hidden_near, hidden_far, motion_near, motion_far,
    gates_ref, cand_ref, out_ref, hidden_rim, motion_rim, reset_pair, cand_pair,
):
    rows, _, ch = hidden_ref.shape
    taps = gates_ref.shape[0]
    tile = out_ref.shape[2]
    half = taps // 2
    rim = 2 * half
    near_below = place_ref[1]
    near, far = rim * near_below, rim - rim * near_below
    here = pl.ds(pl.multiple_of(pl.program_id(0) * tile, tile), tile)
    hidden_rim[pl.ds(near, rim)] = hidden_near[:, here, :]
    hidden_rim[pl.ds(far, rim)] = hidden_far[:, here, :]
    motion_rim[pl.ds(near, rim)] = motion_near[:, here, :]
    motion_rim[pl.ds(far, rim)] = motion_far[:, here, :]

    @pl.when(pl.program_id(0) == 0)
    def _():
        reset_pair[...] = row_pair([gates_ref[t][:, ch:] for t in range(taps)])
        cand_pair[...] = row_pair([cand_ref[t] for t in range(taps)])

    gates = gates_ref[...].reshape(taps * 2 * ch, 2 * ch)

    def row_of(own, rim_ref, y):
        if y < 0:
            return rim_ref[y + rim]
        return own[y, here, :] if y < rows else rim_ref[rim + y - rows]

    state = lambda y: row_of(hidden_ref, hidden_rim, y)
    flow = lambda y: row_of(motion_ref, motion_rim, y)

    def stack(first, last, source):
        return jnp.concatenate(
            [part for y in range(first, last + 1) for part in (source(y), flow(y))], axis=1
        )

    reset_sums, update = {}, []
    for y in (-half, rows):
        both = dotf(stack(y - half, y + half + 1, state), reset_pair[...])
        reset_sums[y], reset_sums[y + 1] = both[:, :ch], both[:, ch:]
    sums = [dotf(stack(y - half, y + half, state), gates) for y in range(rows)]
    for y in range(rows):
        update.append(sigmoid(sums[y][:, :ch]))
        reset_sums[y] = sums[y][:, ch:]
    reset = {
        y: (sigmoid(reset_sums[y]) * state(y).astype(f32)).astype(bf16)
        for y in range(-half, rows + half)
    }
    totals = []
    for y in range(0, rows, 2):
        both = dotf(stack(y - half, y + half + 1, lambda k: reset[k]), cand_pair[...])
        totals += [both[:, :ch], both[:, ch:]]
    for y in range(rows):
        cand = jnp.tanh(totals[y])
        blended = (1.0 - update[y]) * state(y).astype(f32) + update[y] * cand
        out_ref[0, y] = blended.astype(bf16)


def vertical_pass(place, hidden, motion, rims, gates, cand):
    rows, width, ch = hidden.shape
    taps = gates.shape[0]
    rim = rims[0].shape[0]
    tile = 256
    return pl.pallas_call(
        vertical_kernel,
        grid=(width // tile,),
        in_specs=[IN_SMEM] + [IN_VMEM] * 8,
        out_specs=pl.BlockSpec((1, rows, tile, ch), lambda i: (0, 0, i, 0)),
        scratch_shapes=[pltpu.VMEM((2 * rim, tile, ch), bf16)] * 2
        + [pltpu.VMEM(((taps + 1) * 2 * ch, 2 * ch), bf16)] * 2,
        out_shape=jax.ShapeDtypeStruct((1, rows, width, ch), bf16),
        compiler_params=params(24),
        name="vertical",
    )(place, hidden, motion, *rims, gates, cand)


def shards(
    left_feats, right_feats, prev_hidden, warp_list, enc_weight, hgate_w, hcand_w, vgate_w, vcand_w
):
    right = lax.axis_index("cols")
    below = 1 - lax.axis_index("rows") % 2
    place = jnp.stack([right, below]).astype(jnp.int32)
    swap_cols = lambda value: lax.ppermute(value, "cols", [(0, 1), (1, 0)])
    pinned = lax.optimization_barrier

    warp_list = jnp.transpose(warp_list, (0, 2, 3, 1))
    edge = lax.ppermute(right_feats, "cols", [(0, 1)])
    near_list = swap_near(warp_list, "rows")
    far_list = swap_far(warp_list, "rows")
    motion, motion_to_near, motion_to_far = motion_of(
        place, left_feats, right_feats, edge, enc_weight
    )
    near_list, far_list, motion = pinned((near_list, far_list, motion))
    to_near, to_far = gather_blocks(place, near_list, far_list, prev_hidden)
    near = swap_near(to_near, "rows")
    far = swap_far(to_far, "rows")
    motion_near = swap_near(motion_to_near, "rows")
    motion_far = swap_far(motion_to_far, "rows")
    warped, seam = warp_of(place, warp_list, prev_hidden, near, far, motion)
    seam = swap_cols(seam)
    hidden, to_near, to_far = horizontal_pass(place, warped, motion, seam, hgate_w, hcand_w)
    state_near = swap_near(to_near, "rows")
    state_far = swap_far(to_far, "rows")
    rims = (state_near, state_far, motion_near, motion_far)
    return vertical_pass(place, hidden, motion, rims, vgate_w, vcand_w)


def solution(mesh):
    spread = P(("groups", "cams"), "rows", "cols", None)
    return jax.shard_map(
        shards,
        mesh=mesh,
        in_specs=(spread,) * 4 + (P(),) * 5,
        out_specs=spread,
        check_vma=False,
    )
```

time: 119 us -> 62.2 us (0.52)
  Pallas kernels: 75.1 us -> 21.1 us
  local copies, waits for them, and re-layouts: 7.6 us -> 3.37 us
  waiting for transfers between devices: 18.3 us -> 21.1 us
  other arithmetic: 1.93 us -> 0.08 us
    pallas_call x5, Pallas kernels: 75.1 us -> 21.1 us  [the longest x1 7.26 us: vertical_pass(): pl.pallas_call(vertical_kernel, grid=(width // tile,), in_specs=[IN_SMEM]...]
    ppermute x4, waiting for transfers between devices: 11.9 us -> 13.9 us  [swap_near(): return lax.ppermute(value, axis, pairs)]
    slice x2 -> x0, local copies, waits for them, and re-layouts: 1.57 us -> none  [the longest x1 0.79 us: shards(): warped[:, at:at + SEAM]]
    select_n x2 -> x0, other arithmetic: 1.29 us -> none  [the longest x1 1.27 us: shards(): motion_far = swap_far(jnp.where(odd == 0, low, high), 'rows')]
    unnamed x25 -> x18, local copies, waits for them, and re-layouts: 4.26 us -> 3.37 us
  transfers between devices with their start and end apart: 10 -> 10, of which waited for: 6 -> 6; matrix products, arithmetic and copies ran while one was open for 4% -> 0% of each run, Pallas kernels for 36% -> 16%
where the time goes in v1:
time: 62.2 us; the launch traced here: 61.9 us
  waiting for transfers between devices  21.1 us (34%)
  Pallas kernels  21.1 us (34%)
  starting transfers between devices  16.1 us (26%)
  local copies, waits for them, and re-layouts  3.37 us (5%)
    ppermute x4, waiting for transfers between devices, swap_near(): return lax.ppermute(value, axis, pairs)  13.9 us
    ppermute x4, starting transfers between devices, swap_far(): return lax.ppermute(value, axis, pairs)  12 us
    pallas_call x1, Pallas kernels, vertical_pass(): pl.pallas_call(vertical_kernel, grid=(width // tile,), in_specs=[IN_SMEM]...  7.26 us
    ppermute x4, waiting for transfers between devices, swap_far(): return lax.ppermute(value, axis, pairs)  7.16 us
    pallas_call x1, Pallas kernels, horizontal_pass(): pl.pallas_call(horizontal_kernel, in_specs=[IN_SMEM] + [IN_VMEM] * 5, out...  6.38 us
    unnamed x18, local copies, waits for them, and re-layouts  3.37 us
    pallas_call x1, Pallas kernels, motion_of(): pl.pallas_call(motion_kernel, in_specs=[IN_SMEM] + [IN_VMEM] * 4, out_spe...  3.25 us
    pallas_call x1, Pallas kernels, gather_blocks(): pl.pallas_call(gather_kernel, in_specs=[IN_SMEM, IN_VMEM, IN_VMEM, IN_VME...  2.95 us
  transfers between devices with their start and end apart: 10, of which 6 were waited for; matrix products, arithmetic and copies ran while one was open for 0% of the time, Pallas kernels for 16%

profile of v1, /device:TPU:8, one launch (start us, length us, event | category | flops | bytes accessed | tf_op | source)
XLA Modules:
  0.0 61.9 jit_solution(8684764189731680599)
XLA Ops:
  0.0 1.8 %collective-permute-start.2 = (bf16[1,8,512,128]{3,2,1,0:T(8,128)(2,1)}, bf16[1,8,512,128]{3,2,1,0:T(8,128)(2,1)S(1)}, u32[]{:S(2)}, u32[]{:S(2)}) collective-permute-start(bf16[1,8,512,128]{3,2,1,0:T(8,128)(2,1)} %right_ref.1), channel_id=1, source_target_pairs={{0,1},{2,3},{4,5},{6,7},{8,9},{10,11},{12,13},{14,15},{16,17},{18,... | collective-permute-start | bytes 3145736 | tf_op jit(solution)/shard_map/ppermute | solution.py:383
  1.8 3.5 %collective-permute-start.1 = (s32[1,4,4,8]{3,2,1,0:T(4,128)}, s32[1,4,4,8]{3,2,1,0:T(4,128)S(1)}, u32[]{:S(2)}, u32[]{:S(2)}) collective-permute-start(s32[1,4,4,8]{3,2,1,0:T(4,128)} %bitcast.3), channel_id=1, source_target_pairs={{4,8},{8,4},{5,9},{9,5},{6,10},{10,6},{7,11},{11,7},{20,24},{24,20... | collective-permute-start | bytes 1544 | tf_op jit(solution)/shard_map/ppermute | solution.py:34
  5.3 0.1 collective-permute-start
  5.4 0.1 pad_add_fusion.place_ref
  5.5 0.0 copy-start
  5.5 0.0 collective-permute-done.2.edge_ref
  5.5 0.0 copy-start.1
  5.5 1.3 %copy-done.1 = bf16[1,8,512,128]{3,2,1,0:T(8,128)(2,1)S(1)} copy-done((bf16[1,8,512,128]{3,2,1,0:T(8,128)(2,1)S(1)}, bf16[1,8,512,128]{3,2,1,0:T(8,128)(2,1)}, u32[]{:S(2)}) %copy-start.1) | copy-done | bytes 1048600
  6.8 0.0 copy-start.2
  6.8 1.2 %copy-done.2 = bf16[1,8,512,128]{3,2,1,0:T(8,128)(2,1)S(1)} copy-done((bf16[1,8,512,128]{3,2,1,0:T(8,128)(2,1)S(1)}, bf16[1,8,512,128]{3,2,1,0:T(8,128)(2,1)}, u32[]{:S(2)}) %copy-start.2) | copy-done | bytes 1048600
  8.0 0.0 copy-start.7
  8.0 0.8 %copy-done.7 = bf16[192,128]{1,0:T(8,128)(2,1)S(1)} copy-done((bf16[192,128]{1,0:T(8,128)(2,1)S(1)}, bf16[192,128]{1,0:T(8,128)(2,1)}, u32[]{:S(2)}) %copy-start.7) | copy-done | bytes 49176
  8.8 3.3 %motion.1 = (bf16[8,512,128]{2,1,0:T(8,128)(2,1)S(1)}, bf16[4,512,128]{2,1,0:T(8,128)(2,1)S(1)}, bf16[4,512,128]{2,1,0:T(8,128)(2,1)S(1)}) custom-call(s32[2]{0:T(128)S(1)} %pad_add_fusion.place_ref, bf16[1,8,512,128]{3,2,1,0:T(8,128)(2,1)S(1)} %copy-done.1, bf16[1,8,512,128]{3,2,1,0:T(8,128)(2,1)S(1)} %copy-done.2, ...), custom_call_target="tpu_custom_call" | custom-call | tf_op jit(solution)/shard_map/motion/pallas_call | solution.py:104
  12.1 0.0 collective-permute-done.1.far_list
  12.1 0.0 collective-permute-done.near_list
  12.1 0.0 copy-done
  12.1 0.0 copy-start.8
  12.1 3.0 %gather.1 = (bf16[8,128,128]{2,1,0:T(8,128)(2,1)S(1)}, bf16[8,128,128]{2,1,0:T(8,128)(2,1)S(1)}) custom-call(s32[2]{0:T(128)S(1)} %pad_add_fusion.place_ref, s32[1,4,4,8]{3,2,1,0:T(4,128)S(1)} %collective-permute-done.near_list, s32[1,4,4,8]{3,2,1,0:T(4,128)S(1)} %collective-permute-done.1.far_list, bf16[1,8,512,128]{3,2,1,0:T(8,128)(2,1)S(1)} %copy-done), custom_call_target="tpu_custom_call" | custom-call | tf_op jit(solution)/shard_map/gather/pallas_call | solution.py:148
  15.1 2.0 %collective-permute-start.3 = (bf16[8,128,128]{2,1,0:T(8,128)(2,1)S(1)}, bf16[8,128,128]{2,1,0:T(8,128)(2,1)S(1)}, u32[]{:S(2)}, u32[]{:S(2)}) collective-permute-start(bf16[8,128,128]{2,1,0:T(8,128)(2,1)S(1)} %get-tuple-element.21), channel_id=1, source_target_pairs={{0,4},{4,0},{8,12},{12,8},{1,5},{5,1},{9,13},{13,9},{2,6},{6,2},{1... | collective-permute-start | bytes 786440 | tf_op jit(solution)/shard_map/ppermute | solution.py:26
  17.1 0.0 copy-start.4
  17.1 0.0 copy-start.6
  17.1 2.5 %collective-permute-start.4 = (bf16[8,128,128]{2,1,0:T(8,128)(2,1)S(1)}, bf16[8,128,128]{2,1,0:T(8,128)(2,1)S(1)}, u32[]{:S(2)}, u32[]{:S(2)}) collective-permute-start(bf16[8,128,128]{2,1,0:T(8,128)(2,1)S(1)} %get-tuple-element.22), channel_id=1, source_target_pairs={{4,8},{8,4},{5,9},{9,5},{6,10},{10,6},{7,11},{11,7},{20,24},{24,20... | collective-permute-start | bytes 786440 | tf_op jit(solution)/shard_map/ppermute | solution.py:34
  19.6 2.9 %collective-permute-done.3.near_ref = bf16[8,128,128]{2,1,0:T(8,128)(2,1)S(1)} collective-permute-done((bf16[8,128,128]{2,1,0:T(8,128)(2,1)S(1)}, bf16[8,128,128]{2,1,0:T(8,128)(2,1)S(1)}, u32[]{:S(2)}, u32[]{:S(2)}) %collective-permute-start.3) | collective-permute-done | bytes 262176 | tf_op jit(solution)/shard_map/ppermute | solution.py:26
  22.4 3.4 %collective-permute-done.4.far_ref = bf16[8,128,128]{2,1,0:T(8,128)(2,1)S(1)} collective-permute-done((bf16[8,128,128]{2,1,0:T(8,128)(2,1)S(1)}, bf16[8,128,128]{2,1,0:T(8,128)(2,1)S(1)}, u32[]{:S(2)}, u32[]{:S(2)}) %collective-permute-start.4) | collective-permute-done | bytes 262176 | tf_op jit(solution)/shard_map/ppermute | solution.py:34
  25.8 0.0 copy-done.8
  25.8 1.2 %warp.1 = (bf16[8,512,128]{2,1,0:T(8,128)(2,1)S(1)}, bf16[8,16,256]{2,1,0:T(8,128)(2,1)S(1)}) custom-call(s32[2]{0:T(128)S(1)} %pad_add_fusion.place_ref, s32[1,4,4,8]{3,2,1,0:T(4,128)S(1)} %bitcast.5, bf16[1,8,512,128]{3,2,1,0:T(8,128)(2,1)S(1)} %copy-done, bf16[8,128,128]{2,1,0:T(8,128)(2,1)S(1)} %collective-permute-done.3.near_ref, ...), custom_call_target="tpu_custom_call" | custom-call | tf_op jit(solution)/shard_map/warp/pallas_call | solution.py:187
  27.0 0.1 collective-permute-start.5
  27.1 0.1 collective-permute-start.8
  27.2 3.3 %collective-permute-start.9 = (bf16[4,512,128]{2,1,0:T(8,128)(2,1)S(1)}, bf16[4,512,128]{2,1,0:T(8,128)(2,1)S(1)}, u32[]{:S(2)}, u32[]{:S(2)}) collective-permute-start(bf16[4,512,128]{2,1,0:T(8,128)(2,1)S(1)} %get-tuple-element.30), channel_id=1, source_target_pairs={{4,8},{8,4},{5,9},{9,5},{6,10},{10,6},{7,11},{11,7},{20,24},{24,20... | collective-permute-start | bytes 1572872 | tf_op jit(solution)/shard_map/ppermute | solution.py:34
  30.5 0.0 collective-permute-done.5.seam_ref
  30.5 0.0 copy-done.4
  30.5 0.0 copy-done.6
  30.6 0.0 copy-start.3
  30.6 0.0 copy-start.5
  30.6 6.4 %horizontal.1 = (bf16[8,512,128]{2,1,0:T(8,128)(2,1)S(1)}, bf16[4,512,128]{2,1,0:T(8,128)(2,1)S(1)}, bf16[4,512,128]{2,1,0:T(8,128)(2,1)S(1)}) custom-call(s32[2]{0:T(128)S(1)} %pad_add_fusion.place_ref, bf16[8,512,128]{2,1,0:T(8,128)(2,1)S(1)} %get-tuple-element.24.hidden_ref, bf16[8,512,128]{2,1,0:T(8,128)(2,1)S(1)} %get-tuple-element.23.motion_ref, ...), custom_call_target="tpu_custom_call" | custom-call | tf_op jit(solution)/shard_map/horizontal/pallas_call | solution.py:267
  37.0 0.1 collective-permute-start.6
  37.0 2.7 %collective-permute-start.7 = (bf16[4,512,128]{2,1,0:T(8,128)(2,1)S(1)}, bf16[4,512,128]{2,1,0:T(8,128)(2,1)S(1)}, u32[]{:S(2)}, u32[]{:S(2)}) collective-permute-start(bf16[4,512,128]{2,1,0:T(8,128)(2,1)S(1)} %get-tuple-element.28), channel_id=1, source_target_pairs={{4,8},{8,4},{5,9},{9,5},{6,10},{10,6},{7,11},{11,7},{20,24},{24,20... | collective-permute-start | bytes 1572872 | tf_op jit(solution)/shard_map/ppermute | solution.py:34
  39.7 2.2 %collective-permute-done.8.motion_near = bf16[4,512,128]{2,1,0:T(8,128)(2,1)S(1)} collective-permute-done((bf16[4,512,128]{2,1,0:T(8,128)(2,1)S(1)}, bf16[4,512,128]{2,1,0:T(8,128)(2,1)S(1)}, u32[]{:S(2)}, u32[]{:S(2)}) %collective-permute-start.8) | collective-permute-done | bytes 524320 | tf_op jit(solution)/shard_map/ppermute | solution.py:26
  41.9 1.9 %collective-permute-done.9.motion_far = bf16[4,512,128]{2,1,0:T(8,128)(2,1)S(1)} collective-permute-done((bf16[4,512,128]{2,1,0:T(8,128)(2,1)S(1)}, bf16[4,512,128]{2,1,0:T(8,128)(2,1)S(1)}, u32[]{:S(2)}, u32[]{:S(2)}) %collective-permute-start.9) | collective-permute-done | bytes 524320 | tf_op jit(solution)/shard_map/ppermute | solution.py:34
  43.8 8.9 %collective-permute-done.6.hidden_near = bf16[4,512,128]{2,1,0:T(8,128)(2,1)S(1)} collective-permute-done((bf16[4,512,128]{2,1,0:T(8,128)(2,1)S(1)}, bf16[4,512,128]{2,1,0:T(8,128)(2,1)S(1)}, u32[]{:S(2)}, u32[]{:S(2)}) %collective-permute-start.6) | collective-permute-done | bytes 524320 | tf_op jit(solution)/shard_map/ppermute | solution.py:26
  52.7 1.9 %collective-permute-done.7.hidden_far = bf16[4,512,128]{2,1,0:T(8,128)(2,1)S(1)} collective-permute-done((bf16[4,512,128]{2,1,0:T(8,128)(2,1)S(1)}, bf16[4,512,128]{2,1,0:T(8,128)(2,1)S(1)}, u32[]{:S(2)}, u32[]{:S(2)}) %collective-permute-start.7) | collective-permute-done | bytes 524320 | tf_op jit(solution)/shard_map/ppermute | solution.py:34
  54.6 0.0 copy-done.3
  54.6 0.0 copy-done.5
  54.6 7.3 %vertical.1 = bf16[1,8,512,128]{3,2,1,0:T(8,128)(2,1)} custom-call(s32[2]{0:T(128)S(1)} %pad_add_fusion.place_ref, bf16[8,512,128]{2,1,0:T(8,128)(2,1)S(1)} %get-tuple-element.26.hidden_ref, bf16[8,512,128]{2,1,0:T(8,128)(2,1)S(1)} %get-tuple-element.23.motion_ref, bf16[4,512,128]{2,1,0:T(8,128)(2,1)S(1)} %collective-permute-done.6.hidden_near, ...), custom_call_target="tpu_custom_call" | custom-call | tf_op jit(solution)/shard_map/vertical/pallas_call | solution.py:360
Async XLA Ops:
  0.0 5.5 %collective-permute-start.2 = (bf16[1,8,512,128]{3,2,1,0:T(8,128)(2,1)}, bf16[1,8,512,128]{3,2,1,0:T(8,128)(2,1)S(1)}, u32[]{:S(2)}, u32[]{:S(2)}) collective-permute-start(bf16[1,8,512,128]{3,2,1,0:T(8,128)(2,1)} %right_ref.1), channel_id=1, source_target_pairs={{0,1},{2,3},{4,5},{6,7},{8,9},{10,11},{12,13},{14,15},{16,17},{18,... | collective-permute-start | bytes 3145736 | tf_op jit(solution)/shard_map/ppermute | solution.py:383
  1.8 10.3 %collective-permute-start.1 = (s32[1,4,4,8]{3,2,1,0:T(4,128)}, s32[1,4,4,8]{3,2,1,0:T(4,128)S(1)}, u32[]{:S(2)}, u32[]{:S(2)}) collective-permute-start(s32[1,4,4,8]{3,2,1,0:T(4,128)} %bitcast.3), channel_id=1, source_target_pairs={{4,8},{8,4},{5,9},{9,5},{6,10},{10,6},{7,11},{11,7},{20,24},{24,20... | collective-permute-start | bytes 1544 | tf_op jit(solution)/shard_map/ppermute | solution.py:34
  5.3 6.8 %collective-permute-start = (s32[1,4,4,8]{3,2,1,0:T(4,128)}, s32[1,4,4,8]{3,2,1,0:T(4,128)S(1)}, u32[]{:S(2)}, u32[]{:S(2)}) collective-permute-start(s32[1,4,4,8]{3,2,1,0:T(4,128)} %bitcast.4), channel_id=1, source_target_pairs={{0,4},{4,0},{8,12},{12,8},{1,5},{5,1},{9,13},{13,9},{2,6},{6,2},{1... | collective-permute-start | bytes 1544 | tf_op jit(solution)/shard_map/ppermute | solution.py:26
  5.5 6.6 %copy-start = (bf16[1,8,512,128]{3,2,1,0:T(8,128)(2,1)S(1)}, bf16[1,8,512,128]{3,2,1,0:T(8,128)(2,1)}, u32[]{:S(2)}) copy-start(bf16[1,8,512,128]{3,2,1,0:T(8,128)(2,1)} %prev_ref.3) | copy-start | bytes 3145732
  5.5 1.3 %copy-start.1 = (bf16[1,8,512,128]{3,2,1,0:T(8,128)(2,1)S(1)}, bf16[1,8,512,128]{3,2,1,0:T(8,128)(2,1)}, u32[]{:S(2)}) copy-start(bf16[1,8,512,128]{3,2,1,0:T(8,128)(2,1)} %left_ref.1) | copy-start | bytes 3145732
  6.8 1.2 %copy-start.2 = (bf16[1,8,512,128]{3,2,1,0:T(8,128)(2,1)S(1)}, bf16[1,8,512,128]{3,2,1,0:T(8,128)(2,1)}, u32[]{:S(2)}) copy-start(bf16[1,8,512,128]{3,2,1,0:T(8,128)(2,1)} %right_ref.1) | copy-start | bytes 3145732
  8.0 0.8 %copy-start.7 = (bf16[192,128]{1,0:T(8,128)(2,1)S(1)}, bf16[192,128]{1,0:T(8,128)(2,1)}, u32[]{:S(2)}) copy-start(bf16[192,128]{1,0:T(8,128)(2,1)} %weight_ref.1) | copy-start | bytes 147460
  12.1 13.7 %copy-start.8 = (s32[1,8,4,4]{1,3,2,0:T(4,128)S(1)}, s32[1,8,4,4]{1,3,2,0:T(4,128)}, u32[]{:S(2)}) copy-start(s32[1,8,4,4]{1,3,2,0:T(4,128)} %param.12) | copy-start | bytes 1540
  15.1 7.4 %collective-permute-start.3 = (bf16[8,128,128]{2,1,0:T(8,128)(2,1)S(1)}, bf16[8,128,128]{2,1,0:T(8,128)(2,1)S(1)}, u32[]{:S(2)}, u32[]{:S(2)}) collective-permute-start(bf16[8,128,128]{2,1,0:T(8,128)(2,1)S(1)} %get-tuple-element.21), channel_id=1, source_target_pairs={{0,4},{4,0},{8,12},{12,8},{1,5},{5,1},{9,13},{13,9},{2,6},{6,2},{1... | collective-permute-start | bytes 786440 | tf_op jit(solution)/shard_map/ppermute | solution.py:26
  17.1 13.5 %copy-start.4 = (bf16[5,256,256]{2,1,0:T(8,128)(2,1)S(1)}, bf16[5,256,256]{2,1,0:T(8,128)(2,1)}, u32[]{:S(2)}) copy-start(bf16[5,256,256]{2,1,0:T(8,128)(2,1)} %gates_ref.2) | copy-start | bytes 1966084
  17.1 13.5 %copy-start.6 = (bf16[5,256,128]{2,1,0:T(8,128)(2,1)S(1)}, bf16[5,256,128]{2,1,0:T(8,128)(2,1)}, u32[]{:S(2)}) copy-start(bf16[5,256,128]{2,1,0:T(8,128)(2,1)} %cand_ref.2) | copy-start | bytes 983044
  17.1 8.7 %collective-permute-start.4 = (bf16[8,128,128]{2,1,0:T(8,128)(2,1)S(1)}, bf16[8,128,128]{2,1,0:T(8,128)(2,1)S(1)}, u32[]{:S(2)}, u32[]{:S(2)}) collective-permute-start(bf16[8,128,128]{2,1,0:T(8,128)(2,1)S(1)} %get-tuple-element.22), channel_id=1, source_target_pairs={{4,8},{8,4},{5,9},{9,5},{6,10},{10,6},{7,11},{11,7},{20,24},{24,20... | collective-permute-start | bytes 786440 | tf_op jit(solution)/shard_map/ppermute | solution.py:34
  27.0 3.5 %collective-permute-start.5 = (bf16[8,16,256]{2,1,0:T(8,128)(2,1)S(1)}, bf16[8,16,256]{2,1,0:T(8,128)(2,1)S(1)}, u32[]{:S(2)}, u32[]{:S(2)}) collective-permute-start(bf16[8,16,256]{2,1,0:T(8,128)(2,1)S(1)} %get-tuple-element.25), channel_id=1, source_target_pairs={{0,1},{1,0},{2,3},{3,2},{4,5},{5,4},{6,7},{7,6},{8,9},{9,8},{10,11... | collective-permute-start | bytes 196616 | tf_op jit(solution)/shard_map/ppermute | solution.py:379
  27.1 14.8 %collective-permute-start.8 = (bf16[4,512,128]{2,1,0:T(8,128)(2,1)S(1)}, bf16[4,512,128]{2,1,0:T(8,128)(2,1)S(1)}, u32[]{:S(2)}, u32[]{:S(2)}) collective-permute-start(bf16[4,512,128]{2,1,0:T(8,128)(2,1)S(1)} %get-tuple-element.29), channel_id=1, source_target_pairs={{0,4},{4,0},{8,12},{12,8},{1,5},{5,1},{9,13},{13,9},{2,6},{6,2},{1... | collective-permute-start | bytes 1572872 | tf_op jit(solution)/shard_map/ppermute | solution.py:26
  27.2 16.6 %collective-permute-start.9 = (bf16[4,512,128]{2,1,0:T(8,128)(2,1)S(1)}, bf16[4,512,128]{2,1,0:T(8,128)(2,1)S(1)}, u32[]{:S(2)}, u32[]{:S(2)}) collective-permute-start(bf16[4,512,128]{2,1,0:T(8,128)(2,1)S(1)} %get-tuple-element.30), channel_id=1, source_target_pairs={{4,8},{8,4},{5,9},{9,5},{6,10},{10,6},{7,11},{11,7},{20,24},{24,20... | collective-permute-start | bytes 1572872 | tf_op jit(solution)/shard_map/ppermute | solution.py:34
  30.6 24.0 %copy-start.3 = (bf16[5,256,256]{2,1,0:T(8,128)(2,1)S(1)}, bf16[5,256,256]{2,1,0:T(8,128)(2,1)}, u32[]{:S(2)}) copy-start(bf16[5,256,256]{2,1,0:T(8,128)(2,1)} %gates_ref.3) | copy-start | bytes 1966084
  30.6 24.0 %copy-start.5 = (bf16[5,256,128]{2,1,0:T(8,128)(2,1)S(1)}, bf16[5,256,128]{2,1,0:T(8,128)(2,1)}, u32[]{:S(2)}) copy-start(bf16[5,256,128]{2,1,0:T(8,128)(2,1)} %cand_ref.3) | copy-start | bytes 983044
  37.0 15.7 %collective-permute-start.6 = (bf16[4,512,128]{2,1,0:T(8,128)(2,1)S(1)}, bf16[4,512,128]{2,1,0:T(8,128)(2,1)S(1)}, u32[]{:S(2)}, u32[]{:S(2)}) collective-permute-start(bf16[4,512,128]{2,1,0:T(8,128)(2,1)S(1)} %get-tuple-element.27), channel_id=1, source_target_pairs={{0,4},{4,0},{8,12},{12,8},{1,5},{5,1},{9,13},{13,9},{2,6},{6,2},{1... | collective-permute-start | bytes 1572872 | tf_op jit(solution)/shard_map/ppermute | solution.py:26
  37.0 17.5 %collective-permute-start.7 = (bf16[4,512,128]{2,1,0:T(8,128)(2,1)S(1)}, bf16[4,512,128]{2,1,0:T(8,128)(2,1)S(1)}, u32[]{:S(2)}, u32[]{:S(2)}) collective-permute-start(bf16[4,512,128]{2,1,0:T(8,128)(2,1)S(1)} %get-tuple-element.28), channel_id=1, source_target_pairs={{4,8},{8,4},{5,9},{9,5},{6,10},{10,6},{7,11},{11,7},{20,24},{24,20... | collective-permute-start | bytes 1572872 | tf_op jit(solution)/shard_map/ppermute | solution.py:34
